TPU v7x, 256 devices: a whole 4x4x8 slice. The times are simulated.
256 devices in a mesh: tile: 32 (over y, z_hi, core), group: 8 (over z_lo, x).
Axes of the slice: x: 4, y: 4, z: 8 (z_hi: 4, z_lo: 2; z = z_hi * 2 + z_lo), core: 2. Of those that a mesh axis runs over, the one named last changes fastest.
Arguments:
- latents: bfloat16 [1536, 128, 1536], P(('tile', 'group')), may hold values from -6 to 6
- window_index: int32 [3072], P(('tile', 'group')), may hold values from 0 to 2039
- window_len: int32 [3072], P(('tile', 'group')), may hold values from 1 to 64
- live_blocks: int32 [256], P(('tile', 'group')), may hold values from 0 to 6, as said below
- norm_gain: float32 [1536], replicated, may hold values from 0.1 to 1.9
- w_qkv: bfloat16 [1536, 4608], P('group', 'tile'), may hold values from -0.15625 to 0.15625
- w_out: bfloat16 [1536, 1536], P('group', 'tile'), may hold values from -0.15625 to 0.15625
Outputs:
- refined: bfloat16 [1536, 128, 1536], P(('tile', 'group'))
Inputs may be any that keep to these rules, and one draw needn't show every extreme that they name: `live_blocks`: the device at tile index i and the device at tile index i + 16 in the same group form a pair; at most one of a pair holds more than 4 live blocks, the two hold at most 8 together, and in every draw some pair holds exactly 6 and 2.
All inputs are finite; a program needn't handle non-finite values.
Results may differ from a plain program's by a relative error of at most 0.0033.
Values may be sent and summed in bfloat16 or wider, within the bound.
A program may use at most 128 MiB of HBM per device.

v0:
```python
import math

import jax
import jax.numpy as jnp
from jax import lax
from jax.sharding import PartitionSpec as P

D = 1536
HEADS = 24
HEAD_DIM = 64
WIN_SIDE = 8
WIN_COLS = 60
WIN_TOK = 64


def position_table(window_ids):
    token_ids = jnp.arange(WIN_TOK, dtype=jnp.int32)
    row_pos = window_ids[:, None] // WIN_COLS * WIN_SIDE + token_ids[None, :] // WIN_SIDE
    col_pos = window_ids[:, None] % WIN_COLS * WIN_SIDE + token_ids[None, :] % WIN_SIDE
    quarter = D // 4
    frequency = jnp.exp(jnp.arange(quarter, dtype=jnp.float32) * (-math.log(10000.0) / quarter))
    row_angle = row_pos.astype(jnp.float32)[:, :, None] * frequency
    col_angle = col_pos.astype(jnp.float32)[:, :, None] * frequency
    return jnp.concatenate(
        [jnp.sin(row_angle), jnp.cos(row_angle), jnp.sin(col_angle), jnp.cos(col_angle)], axis=-1
    )


def head_norm(values):
    return (values * lax.rsqrt(jnp.mean(values * values, axis=-1, keepdims=True) + 1e-06)).astype(
        jnp.bfloat16
    )


def project_qkv(normed, w_qkv):
    full_rows = lax.all_gather(w_qkv, "group", axis=0, tiled=True)
    return jnp.dot(
        normed,
        lax.all_gather(full_rows, "tile", axis=1, tiled=True),
        preferred_element_type=jnp.float32,
    )


def window_layer(blocks_in, window_ids, window_lens, norm_gain, w_qkv, w_out):
    window_count = window_ids.shape[0]
    stream = blocks_in.reshape(window_count, WIN_TOK, D).astype(jnp.float32) + position_table(
        window_ids
    )
    scale = lax.rsqrt(jnp.mean(stream * stream, axis=-1, keepdims=True) + 1e-06)
    normed = (stream * scale * norm_gain).astype(jnp.bfloat16).reshape(window_count * WIN_TOK, D)
    projected = project_qkv(normed, w_qkv)
    projected = projected.reshape(window_count, WIN_TOK, 3, HEADS, HEAD_DIM)
    queries = head_norm(projected[:, :, 0])
    keys = head_norm(projected[:, :, 1])
    values = projected[:, :, 2].astype(jnp.bfloat16)
    scores = jnp.einsum(
        "wqhd,wkhd->whqk", queries, keys, preferred_element_type=jnp.float32
    ) * HEAD_DIM ** (-0.5)
    key_mask = jnp.arange(WIN_TOK, dtype=jnp.int32)[None, :] < window_lens[:, None]
    weights = jnp.exp(scores) * key_mask[:, None, None, :].astype(jnp.float32)
    probs = (weights / jnp.sum(weights, axis=-1, keepdims=True)).astype(jnp.bfloat16)
    attended = jnp.einsum("whqk,wkhd->wqhd", probs, values, preferred_element_type=jnp.float32)
    attended = attended.astype(jnp.bfloat16).reshape(window_count * WIN_TOK, D)
    out_full_rows = lax.all_gather(w_out, "group", axis=0, tiled=True)
    update = jnp.dot(
        attended,
        lax.all_gather(out_full_rows, "tile", axis=1, tiled=True),
        preferred_element_type=jnp.float32,
    )
    base = blocks_in.reshape(window_count * WIN_TOK, D).astype(jnp.float32)
    token_live = key_mask.reshape(window_count * WIN_TOK)[:, None]
    return jnp.where(token_live, base + update, base).astype(jnp.bfloat16).reshape(blocks_in.shape)


def local(latents, window_index, window_len, live_blocks, norm_gain, w_qkv, w_out):
    slot_total = latents.shape[0]
    slot_ids = jnp.arange(slot_total, dtype=jnp.int32)
    live_mask = (slot_ids < live_blocks[0])[:, None, None]
    finished = window_layer(latents, window_index, window_len, norm_gain, w_qkv, w_out)
    return jnp.where(live_mask, finished, latents)


def solution(mesh):
    in_specs = (
        P(("tile", "group"), None, None),
        P(("tile", "group")),
        P(("tile", "group")),
        P(("tile", "group")),
        P(),
        P("group", "tile"),
        P("group", "tile"),
    )
    out_specs = P(("tile", "group"), None, None)
    return jax.shard_map(local, mesh=mesh, in_specs=in_specs, out_specs=out_specs, check_vma=False)
```

profile of v0, /device:TPU:39, one launch (start us, length us, event | category | flops | bytes accessed | tf_op | source)
XLA Modules:
  0.0 240.5 jit_solution(4403751258433030847)
XLA Ops:
  6.5 23.8 %all-gather = bf16[8,192,144]{1,2,0:T(8,128)(2,1)S(1)} all-gather(bf16[1,192,144]{1,2,0:T(8,128)(2,1)} %bitcast.54), channel_id=1, replica_groups=mesh['tile'=32,'group'=8] {'group'}, dimensions={0}, use_global_device_ids=true | all-gather | bytes 497664 | tf_op jit(solution)/shard_map/all_gather | solution.py:36
  30.3 0.2 copy.17
  30.5 1.2 reshape.310
  31.8 22.1 %all-gather.1 = bf16[8,192,48]{1,2,0:T(8,128)(2,1)S(1)} all-gather(bf16[1,192,48]{1,2,0:T(8,128)(2,1)} %bitcast.55), channel_id=1, replica_groups=mesh['tile'=32,'group'=8] {'group'}, dimensions={0}, use_global_device_ids=true | all-gather | bytes 165888 | tf_op jit(solution)/shard_map/all_gather | solution.py:64
  54.0 0.1 copy.22
  54.0 0.8 reshape.312
  54.9 0.7 fusion.13
  55.6 0.1 add.122
  55.7 0.1 add.123
  55.7 0.1 add.124
  55.8 0.1 add.130
  55.9 0.1 add.131
  56.0 0.1 add.132
  56.1 0.1 add.126
  56.1 0.1 add.135
  56.2 0.7 iota_compare_fusion
  57.6 9.7 %multiply_sine_fusion.1 = (f32[6,128,384]{2,1,0:T(8,128)S(1)}, f32[6,128,384]{2,1,0:T(8,128)}, f32[6,128,384]{2,1,0:T(8,128)}, f32[6,128,384]{2,1,0:T(8,128)S(1)}) fusion(f32[384]{0:T(512)S(1)} %multiply_exponential_fusion, f32[6,128]{1,0:T(8,128)S(1)} %get-tuple-element.20, f32[6,128]{1,0:T(8,128)S(1)} %get-tuple-element.19), kind=kLoop, calls=%fused_computation.27 | loop fusion | flops 589824 | bytes 4726272 | tf_op jit(solution)/shard_map/sin | solution.py:25
  67.3 1.0 copy-done.3
  68.3 2.1 multiply_reduce_fusion.2
  70.4 0.5 iota_compare_fusion.1
  70.9 0.7 lt.51
  71.6 3.4 %multiply_convert_fusion.4 = bf16[6,128,1536]{2,1,0:T(8,128)(2,1)} fusion(f32[1536]{0:T(1024)} %param.11, f32[6,128]{1,0:T(8,128)S(1)} %add_rsqrt_fusion.2, f32[6,128,384]{2,1,0:T(8,128)} %get-tuple-element.11, f32[6,128,384]{2,1,0:T(8,128)} %copy-done.3, f32[6,128,384]{2,1,0:T(8,128)} %get-tuple-element.8, f32[6,128,384]{2,1,0:T(8,128)S(1)} %get-tuple-element.7, ...), kind=kLoop, calls=%fused_computation.21 | loop fusion | flops 9437184 | bytes 9446400 | tf_op jit(solution)/shard_map/convert_element_type | solution.py:50
  74.9 71.5 %all-gather.5.cloned.1.call-done = bf16[1536,4608]{0,1:T(8,128)(2,1)} async-done(((bf16[1536,144]{0,1:T(8,128)(2,1)}), bf16[1536,4608]{0,1:T(8,128)(2,1)}) %all-gather.5.cloned.1.call-update) | async-done | bytes 14155792 | tf_op jit(solution)/shard_map/all_gather | solution.py:39
  146.4 26.0 %fusion.16 = f32[12,64,3,24,64]{1,4,3,2,0:T(8,128)S(1)} fusion(bf16[12,64,1536,1,1]{2,1,4,3,0:T(8,128)(2,1)} %bitcast.52, bf16[3,24,64,1536,1]{3,2,1,0,4:T(8,128)(2,1)} %bitcast.56), kind=kOutput, calls=%fused_computation.47 | convolution fusion | flops 10871635968 | bytes 30670848 | tf_op jit(solution)/shard_map/dot_general | solution.py:37
  172.4 9.3 %copy-done = f32[12,64,3,24,64]{1,4,3,2,0:T(8,128)} copy-done((f32[12,64,3,24,64]{1,4,3,2,0:T(8,128)}, f32[12,64,3,24,64]{1,4,3,2,0:T(8,128)S(1)}, u32[]{:S(2)}) %copy-start) | copy-done | bytes 14155800
  181.8 4.0 %multiply_reduce_fusion.1 = (f32[12,64,24]{1,2,0:T(8,128)S(1)}, f32[12,64,24]{1,2,0:T(8,128)S(1)}) fusion(f32[12,64,3,24,64]{1,4,3,2,0:T(8,128)S(1)} %fusion.16), kind=kLoop, calls=%fused_computation.8 | loop fusion | flops 4681728 | bytes 9584640 | tf_op jit(solution)/shard_map/reduce_sum | solution.py:30
  185.8 13.7 %fusion = (f32[12,24,64]{2,1,0:T(8,128)S(1)}, f32[12,24,64,64]{2,3,1,0:T(8,128)}) fusion(f32[12,64]{1,0:T(8,128)S(1)} %get-tuple-element.14, f32[12,64,3,24,64]{1,4,3,2,0:T(8,128)} %copy-done, f32[12,64,24]{1,2,0:T(8,128)S(1)} %add_rsqrt_fusion, f32[12,64,24]{1,2,0:T(8,128)S(1)} %add_rsqrt_fusion.1), kind=kOutput, calls=%fused_computation.9 | convolution fusion | flops 159234048 | bytes 23817216 | tf_op jit(solution)/shard_map/wqhd,wkhd->whqk/dot_general | solution.py:56
  199.5 11.1 %convert_bitcast_fusion = bf16[12,64,24,64]{1,3,2,0:T(8,128)(2,1)} fusion(f32[12,24,64,64]{2,3,1,0:T(8,128)} %get-tuple-element.18, f32[12,24,64]{2,1,0:T(8,128)S(1)} %get-tuple-element.17, f32[12,64]{1,0:T(8,128)S(1)} %get-tuple-element.14, f32[12,64,3,24,64]{1,4,3,2,0:T(8,128)} %copy-done), kind=kOutput, calls=%fused_computation.16 | convolution fusion | flops 156893184 | bytes 16591872 | tf_op jit(solution)/shard_map/whqk,wkhd->wqhd/dot_general | solution.py:62
  210.7 6.9 %copy.21 = bf16[12,64,24,64]{3,2,1,0:T(8,128)(2,1)} copy(bf16[12,64,24,64]{1,3,2,0:T(8,128)(2,1)} %convert_bitcast_fusion) | data formatting | bytes 4718592 | tf_op jit(solution)/shard_map/convert_element_type | solution.py:63
  217.6 7.4 %reshape.306 = bf16[768,1536]{1,0:T(8,128)(2,1)} reshape(bf16[12,64,24,64]{3,2,1,0:T(8,128)(2,1)} %copy.21) | data formatting | bytes 4718592 | tf_op jit(solution)/shard_map/reshape | solution.py:63
  225.0 6.9 %fusion.1 = bf16[768,1536]{1,0:T(8,128)(2,1)S(1)} fusion(bf16[768,1536]{1,0:T(8,128)(2,1)} %reshape.306, bf16[1536,1536]{0,1:T(8,128)(2,1)} %all-gather.7.cloned.1.call-done, pred[768]{0:T(1024)(128)(4,1)S(1)} %copy-done.4, bf16[6,128,1536]{2,1,0:T(8,128)(2,1)S(1)} %copy-done.2), kind=kOutput, calls=%fused_computation.11 | convolution fusion | flops 3628597248 | bytes 11797248 | tf_op jit(solution)/shard_map/dot_general | solution.py:65
  231.9 1.7 broadcast_select_fusion
  (24 shorter events, 0.2 us)
Async XLA Ops:
  6.5 61.8 %copy-start.1 = (bf16[6,128,1536]{2,1,0:T(8,128)(2,1)S(1)}, bf16[6,128,1536]{2,1,0:T(8,128)(2,1)}, u32[]{:S(2)}) copy-start(bf16[6,128,1536]{2,1,0:T(8,128)(2,1)} %param.7) | copy-start | bytes 7077892
  6.5 139.9 %all-gather.5.cloned.1.call-start = ((), (), s32[]{:S(2)}) async-start(), calls=%async_computation | async-start | bytes 14598144 | tf_op jit(solution)/shard_map/all_gather | solution.py:39
  31.8 193.2 %all-gather.7.cloned.1.call-start = ((), (), s32[]{:S(2)}) async-start(), calls=%async_computation.1 | async-start | bytes 4866048 | tf_op jit(solution)/shard_map/all_gather | solution.py:67
  67.3 1.0 copy-start.3
  172.4 9.4 %copy-start = (f32[12,64,3,24,64]{1,4,3,2,0:T(8,128)}, f32[12,64,3,24,64]{1,4,3,2,0:T(8,128)S(1)}, u32[]{:S(2)}) copy-start(f32[12,64,3,24,64]{1,4,3,2,0:T(8,128)S(1)} %fusion.16) | copy-start | bytes 42467332
  217.6 7.4 %copy-start.2 = (bf16[6,128,1536]{2,1,0:T(8,128)(2,1)S(1)}, bf16[6,128,1536]{2,1,0:T(8,128)(2,1)}, u32[]{:S(2)}) copy-start(bf16[6,128,1536]{2,1,0:T(8,128)(2,1)} %param.7) | copy-start | bytes 7077892
  217.6 7.4 %copy-start.4 = (pred[768]{0:T(1024)(128)(4,1)S(1)}, pred[768]{0:T(1024)(128)(4,1)}, u32[]{:S(2)}) copy-start(pred[768]{0:T(1024)(128)(4,1)} %lt.51) | copy-start | bytes 2308
  225.0 6.9 %copy-start.5 = (pred[6]{0:T(512)(128)(4,1)S(1)}, pred[6]{0:T(512)(128)(4,1)}, u32[]{:S(2)}) copy-start(pred[6]{0:T(512)(128)(4,1)} %iota_compare_fusion.1) | copy-start | bytes 22
Sparse Core Ops, SparseCore 0:
  31.9 114.5 all-gather.4
  149.0 58.9 all-gather.6
where the time goes:
time: 241 us; the launch traced here: 240 us
  waiting for transfers between devices  71.6 us (30%)
  matrix products  57.7 us (24%)
  blocking collectives  45.9 us (19%)
  local copies, waits for them, and re-layouts  28.3 us (12%)
  other arithmetic  22.8 us (9%)
  between operations  14.2 us (6%)
    all_gather x1, waiting for transfers between devices, project_qkv(): lax.all_gather(full_rows, 'tile', axis=1, tiled=True)  71.5 us
    dot_general x1, matrix products, project_qkv(): jnp.dot(normed, lax.all_gather(full_rows, 'tile', axis=1, tiled=True), pr...  26 us
    all_gather x1, blocking collectives, project_qkv(): full_rows = lax.all_gather(w_qkv, 'group', axis=0, tiled=True)  23.8 us
    all_gather x1, blocking collectives, window_layer(): out_full_rows = lax.all_gather(w_out, 'group', axis=0, tiled=True)  22.1 us
    dot_general x1, matrix products, window_layer(): jnp.einsum('wqhd,wkhd->whqk', queries, keys, preferred_element_type=jnp.f...  13.7 us
    unnamed x14, local copies, waits for them, and re-layouts  12.5 us
    dot_general x1, matrix products, window_layer(): jnp.einsum('whqk,wkhd->wqhd', probs, values, preferred_element_type=jnp.f...  11.1 us
    sin x1, other arithmetic, position_table(): jnp.sin(row_angle)  9.65 us
  transfers between devices with their start and end apart: 2, of which 1 were waited for; matrix products, arithmetic and copies ran while one was open for 37% of the time, Pallas kernels for 0%

commit v1 on v0

v1 whole, which is shorter than its diff:
```python
import math
import heapq

import jax
import jax.numpy as jnp
from jax import lax
from jax.experimental import pallas as pl
from jax.experimental.pallas import tpu as pltpu
from jax.sharding import PartitionSpec as P

D = 1536
HEAD_DIM = 64
WIN_SIDE = 8
WIN_COLS = 60
WIN_TOK = 64
SLOTS = 6
BLOCK = 128
TOK = SLOTS * BLOCK
PART = 96
LANES = 128
FULL = "F"
AXLEN = {"x": 4, "y": 4, "z": 8}
AXPOS = {"x": 0, "y": 1, "z": 2}
MESH = pl.DeviceIdType.MESH


def moved(region, axis, step):
    pos = AXPOS[axis]
    n = AXLEN[axis]
    out = list(region)
    out[pos] = (region[pos] - step) % n
    return tuple(out)

def plan():
    rate = 46.5e3
    free = {}
    queue = []
    order = []
    have = {}
    count = [0]
    seq = [0]

    def bytes_of(color, region, half):
        n = PART * 256
        for r in region:
            if r == FULL:
                n *= 4
        return n // 2 if half else n

    def send(now, color, region, axis, step, half=None):
        n = AXLEN[axis]
        hops = min(step, n - step)
        sign = 1 if step <= n // 2 else -1
        link = (axis, sign)
        start = max(now, free.get(link, 0.0))
        end = start + hops * bytes_of(color, region, half) / rate
        free[link] = end
        ident = count[0]
        count[0] += 1
        seq[0] += 1
        heapq.heappush(queue, (end + 1.0 + 0.75 * hops, seq[0], ident, color, moved(region, axis, step), half))
        return (ident, color, region, axis, step, half)

    def complete(now, color, region, out):
        rx, ry, rz = region
        if color == "A":
            if region == (0, 0, 0):
                for s in (1, 3, 2):
                    out.append(send(now, "A", region, "x", s))
                return
            if rz == 0 and ry == 0 and rx != FULL:
                if all(((k, 0, 0) in have["A"]) for k in (1, 2, 3)):
                    complete(now, "A", (FULL, 0, 0), out)
                return
            if rz == 0:
                if ry == 0:
                    out.append(send(now, "A", region, "y", 1))
                    out.append(send(now, "A", region, "y", 3))
                elif ry == 3:
                    out.append(send(now, "A", region, "y", 1, 0))
                elif ry == 1:
                    out.append(send(now, "A", region, "y", 3, 1))
                out.append(send(now, "A", region, "z", 1))
                out.append(send(now, "A", region, "z", 7))
            elif rz >= 5:
                out.append(send(now, "A", region, "z", 1, 0 if rz == 5 else None))
            elif rz <= 3:
                out.append(send(now, "A", region, "z", 7, 1 if rz == 3 else None))
            have["A", rz] = have.get(("A", rz), 0) + 1
            if have["A", rz] == 4:
                out.append(("sib", "A", (FULL, FULL, rz)))
            return
        mid, last = ("y", "x") if color == "B" else ("x", "y")
        m, l = AXPOS[mid], AXPOS[last]
        if region[m] != FULL and region[l] == 0:
            if region[m] == 0:
                if rz == 0:
                    out.append(send(now, color, region, "z", 1))
                    out.append(send(now, color, region, "z", 7))
                elif rz in (7, 6) or (rz == 5 and color == "B"):
                    out.append(send(now, color, region, "z", 1))
                elif rz in (1, 2) or (rz == 3 and color == "C"):
                    out.append(send(now, color, region, "z", 7))
                out.append(send(now, color, region, mid, 1))
                out.append(send(now, color, region, mid, 3))
            elif region[m] == 3 and rz % 2 == 0:
                out.append(send(now, color, region, mid, 1))
            elif region[m] == 1 and rz % 2 == 1:
                out.append(send(now, color, region, mid, 3))
            parts = []
            for k in range(4):
                r = list(region)
                r[m] = k
                parts.append(tuple(r) in have[color])
            if all(parts):
                r = list(region)
                r[m] = FULL
                complete(now, color, tuple(r), out)
            return
        if region[l] == 0:
            out.append(send(now, color, region, last, 1))
            out.append(send(now, color, region, last, 3))
        elif region[l] == 3:
            out.append(send(now, color, region, last, 1, 0))
        elif region[l] == 1:
            out.append(send(now, color, region, last, 3, 1))
        key = (color, region[l])
        have[key] = have.get(key, 0) + 1
        if have[key] == 8:
            out.append(("sib", color, (region[0], region[1], FULL)))

    first = []
    for color in "BCA":
        have[color] = {(0, 0, 0)}
        complete(0.0, color, (0, 0, 0), first)
    order.append((None, first))
    end = 0.0
    while queue:
        now, _, ident, color, region, half = heapq.heappop(queue)
        end = now
        out = []
        if half is None:
            have[color].add(region)
            complete(now, color, region, out)
        else:
            got = have[color]
            got.add((region, half))
            if (region, 1 - half) in got:
                got.add(region)
                complete(now, color, region, out)
        order.append(((ident, color, region, half), out))
    return order, count[0], end

def parts_of(ref_f, ref_r, color):
    if color == "A":
        return ref_r
    return ref_f.at[pl.ds(0 if color == "B" else PART, PART), :]


def gather_weights(src_f, src_r, wf, wr, send_sem, recv_sem, sib_sem, loc_sem, meanwhile=None):
    tile = lax.axis_index("tile"); group = lax.axis_index("group")
    y = tile // 8; zh = (tile // 2) % 4; c = tile % 2
    zl = group // 4; x = group % 4
    z = zh * 2 + zl

    xs = [x] + [(x + k) % 4 for k in (1, 2, 3)]
    ys = [y] + [(y + k) % 4 for k in (1, 2, 3)]
    zs = [(zl, zh)] + [(((z + k) % 8) % 2, ((z + k) % 8) // 2) for k in range(1, 8)]

    def dev_of(axis, step):
        xx, yy, zz, cc = x, y, zs[0], c
        if axis == "x": xx = xs[step]
        if axis == "y": yy = ys[step]
        if axis == "z": zz = zs[step]
        if axis == "c": cc = 1 - c
        return (yy * 8 + zz[1] * 2 + cc, zz[0] * 4 + xx)
    table = {}
    def dev(axis, step):
        if (axis, step) not in table:
            table[axis, step] = dev_of(axis, step)
        return table[axis, step]

    bar = pltpu.get_barrier_semaphore()
    peers = [("x", 1), ("x", 3), ("x", 2), ("y", 1), ("y", 3), ("z", 1), ("z", 7), ("c", 1)]
    for p in peers:
        pl.semaphore_signal(bar, inc=1, device_id=dev(*p), device_id_type=MESH)
    pl.semaphore_wait(bar, len(peers))

    own_f = wf.at[zl, x, y, zh, c]
    own_r = wr.at[zl, x, y, zh, c]
    loc_f = pltpu.make_async_copy(src_f, own_f, loc_sem.at[0])
    loc_r = pltpu.make_async_copy(src_r, own_r, loc_sem.at[1])
    loc_f.start()
    loc_r.start()

    def view(color, region, half=None, core=None):
        rx, ry, rz = region
        part = pl.ds(0, 4) if half is None else pl.ds(2 * half, 2)
        ix = part if rx == FULL else xs[rx]
        iy = part if ry == FULL else ys[ry]
        iz = (pl.ds(0, 2), pl.ds(0, 4)) if rz == FULL else zs[rz]
        cc = c if core is None else core
        if color == "A":
            return wr.at[iz[0], ix, iy, iz[1], cc]
        return wf.at[iz[0], ix, iy, iz[1], cc, pl.ds(0 if color == "B" else PART, PART), :]

    order, total, end = plan()
    sends, sibs = [], []
    def issue(item):
        if item[0] == "sib":
            _, color, region = item
            i = len(sibs)
            ref = view(color, region)
            cp = pltpu.make_async_remote_copy(src_ref=ref, dst_ref=ref, send_sem=sib_sem.at[0, i], recv_sem=sib_sem.at[1, i],
                                              device_id=dev("c", 1), device_id_type=MESH)
            sibs.append((cp, color, region))
        else:
            ident, color, region, axis, step, half = item
            if region == (0, 0, 0):
                ref = parts_of(src_f, src_r, color)
                dst = parts_of(own_f, own_r, color)
            else:
                ref = dst = view(color, region, half)
            cp = pltpu.make_async_remote_copy(src_ref=ref, dst_ref=dst, send_sem=send_sem.at[ident], recv_sem=recv_sem.at[ident],
                                              device_id=dev(axis, step), device_id_type=MESH)
            sends.append(cp)
        cp.start()
    for n, (arrival, out) in enumerate(order):
        if arrival is not None:
            ident, color, region, half = arrival
            ref = view(color, region, half)
            pltpu.make_async_remote_copy(src_ref=ref, dst_ref=ref, send_sem=send_sem.at[ident], recv_sem=recv_sem.at[ident],
                                         device_id=dev("c", 1), device_id_type=MESH).wait_recv()
        for item in out:
            issue(item)
        if n == 0:
            loc_f.wait()
            loc_r.wait()
            if meanwhile is not None:
                meanwhile()
    for i, (cp, color, region) in enumerate(sibs):
        ref = view(color, region, None, 1 - c)
        pltpu.make_async_remote_copy(src_ref=ref, dst_ref=ref, send_sem=sib_sem.at[0, i], recv_sem=sib_sem.at[1, i],
                                     device_id=dev("c", 1), device_id_type=MESH).wait_recv()
    for cp in sends:
        cp.wait_send()
    for cp, _, _ in sibs:
        cp.wait_send()


def window_tables(window_index):
    side = jnp.arange(WIN_SIDE, dtype=jnp.int32)
    rows = (window_index // WIN_COLS * WIN_SIDE)[:, None] + side
    cols = (window_index % WIN_COLS * WIN_SIDE)[:, None] + side
    quarter = D // 4
    frequency = jnp.exp(jnp.arange(quarter, dtype=jnp.float32) * (-math.log(10000.0) / quarter))
    angle = jnp.stack([rows, cols]).astype(jnp.float32)[..., None] * frequency
    return jnp.concatenate([jnp.sin(angle), jnp.cos(angle)], axis=-1)


def norm_tokens(lat, tables, gain, xs_ref):
    def block(b, carry):
        for h in range(2):
            rows = pl.ds(pl.multiple_of(b * BLOCK + h * WIN_TOK, WIN_TOK), WIN_TOK)
            win = 2 * b + h
            tok = lat[rows, :].astype(jnp.float32)
            half = D // 2
            left = tok[:, :half].reshape(8, 8, half) + tables[0, win][:, None, :]
            right = tok[:, half:].reshape(8, 8, half) + tables[1, win][None]
            stream = jnp.concatenate([left.reshape(WIN_TOK, half), right.reshape(WIN_TOK, half)], axis=1)
            scale = lax.rsqrt(jnp.mean(stream * stream, axis=-1, keepdims=True) + 1e-06)
            xs_ref[rows, :] = (stream * scale * gain[...]).astype(jnp.bfloat16)
        return carry

    lax.fori_loop(0, SLOTS, block, 0)


def coords(t):
    return t // 8, (t // 2) % 4, t % 2


def unpack_rest(wr, wu):
    lane = lax.broadcasted_iota(jnp.int32, (PART, LANES), 1) < 64

    def one(t, carry):
        y, zh, c = coords(t)
        for j in range(4):
            zl, x = j // 2, (j % 2) * 2
            even = wr[zl, x, y, zh, c].astype(jnp.float32)
            odd = wr[zl, x + 1, y, zh, c].astype(jnp.float32)
            low = jnp.where(lane, even, odd).astype(jnp.bfloat16)
            high = pltpu.roll(jnp.where(lane, odd, even), 64, 1).astype(jnp.bfloat16)
            for i in range(6):
                wu[j, y, zh, c, 32 * i:32 * i + 16, :] = low[16 * i:16 * i + 16]
                wu[j, y, zh, c, 32 * i + 16:32 * i + 32, :] = high[16 * i:16 * i + 16]
        return carry

    lax.fori_loop(0, 32, one, 0)


def column_tile(wf, wu, groups):
    spots = []
    for t, r in groups:
        spots.append(coords(t) + (pl.ds(pl.multiple_of(r, 16), 16),))
    tiles = []
    for k in range(12):
        j, kind = k // 3, k % 3
        if kind == 1:
            pieces = [wu[j, y, zh, c, rows, :] for y, zh, c, rows in spots]
        else:
            zl, x = j // 2, (j % 2) * 2 + kind // 2
            pieces = [wf[zl, x, y, zh, c, rows, :] for y, zh, c, rows in spots]
        tiles.append(jnp.concatenate(pieces, axis=0))
    return jnp.concatenate(tiles, axis=1)


NT = (((1,), (1,)), ((), ()))


def project(xs_ref, wf, wu, qkv):
    r = lax.broadcasted_iota(jnp.int32, (256, 256), 0) // HEAD_DIM
    c = lax.broadcasted_iota(jnp.int32, (256, 256), 1) // HEAD_DIM
    ones = jnp.where(r == c, 1.0, 0.0).astype(jnp.bfloat16)

    def tile(n, carry):
        groups = []
        for i in range(16):
            g = n * 16 + i
            groups.append((g // 9, (g % 9) * 16))
        p = lax.dot_general(xs_ref[...], column_tile(wf, wu, groups), NT, preferred_element_type=jnp.float32)
        total = jnp.dot((p * p).astype(jnp.bfloat16), ones, preferred_element_type=jnp.float32)
        extra = jnp.where(n < 6, HEAD_DIM ** -0.5, 1.0)
        factor = jnp.where(n < 12, lax.rsqrt(total * (1.0 / HEAD_DIM) + 1e-06) * extra, 1.0)
        qkv[n] = (p * factor).astype(jnp.bfloat16)
        return carry

    lax.fori_loop(0, 18, tile, 0)


def attend(qkv, lens, att):
    lane = lax.broadcasted_iota(jnp.int32, (BLOCK, LANES), 1) < 64
    key = lax.broadcasted_iota(jnp.int32, (BLOCK, 256), 1) % BLOCK
    query = lax.broadcasted_iota(jnp.int32, (BLOCK, 256), 0)
    one = jnp.where(lane, 1.0, 0.0).astype(jnp.bfloat16)
    sums = jnp.concatenate([one, 1.0 - one], axis=0).astype(jnp.bfloat16)

    def block(b, carry):
        rows = pl.ds(pl.multiple_of(b * BLOCK, BLOCK), BLOCK)
        first, second = lens[2 * b], lens[2 * b + 1]
        low = jnp.where(query < 64, 0, 64)
        high = jnp.where(query < 64, first, 64 + second)
        mask = jnp.where(key >= low, 1.0, 0.0) * jnp.where(key < high, 1.0, 0.0)

        def pair(h, inner):
            for part in range(2):
                cols = slice(part * LANES, part * LANES + LANES)
                q = qkv[h, rows, cols]
                k = qkv[6 + h, rows, cols]
                v = qkv[12 + h, rows, cols]
                zero = jnp.zeros_like(k)
                keys = jnp.concatenate([jnp.where(lane, k, zero), jnp.where(lane, zero, k)], axis=0)
                vals = jnp.concatenate([jnp.where(lane, v, zero), jnp.where(lane, zero, v)], axis=0)
                scores = lax.dot_general(q, keys, NT, preferred_element_type=jnp.float32)
                weights = (jnp.exp(scores) * mask).astype(jnp.bfloat16)
                mixed = jnp.dot(weights, jnp.concatenate([vals, sums], axis=1), preferred_element_type=jnp.float32)
                att[h, rows, cols] = (mixed[:, :LANES] / mixed[:, LANES:]).astype(jnp.bfloat16)
            return inner

        lax.fori_loop(0, 6, pair, 0)
        return carry

    lax.fori_loop(0, SLOTS, block, 0)


def finish(att, wf, wu, lat, lens, live, out):
    tok = lax.broadcasted_iota(jnp.int32, (BLOCK, 256), 0)

    def tile(n, carry):
        groups = []
        for i in range(16):
            g = n * 16 + i
            groups.append((g // 3, 144 + (g % 3) * 16))
        wide = jnp.concatenate([att[h] for h in range(6)], axis=1)
        update = lax.dot_general(wide, column_tile(wf, wu, groups), NT, preferred_element_type=jnp.float32)
        cols = pl.ds(pl.multiple_of(n * 256, 256), 256)
        for b in range(SLOTS):
            base = lat[b * BLOCK:(b + 1) * BLOCK, cols].astype(jnp.float32)
            first, second = lens[2 * b], lens[2 * b + 1]
            limit = jnp.where(tok < 64, first, 64 + second)
            limit = jnp.where(b < live[0], limit, 0)
            moved_rows = update[b * BLOCK:(b + 1) * BLOCK]
            out[b * BLOCK:(b + 1) * BLOCK, cols] = jnp.where(tok < limit, base + moved_rows, base).astype(jnp.bfloat16)
        return carry

    lax.fori_loop(0, 6, tile, 0)


def pack(w_qkv, w_out):
    cols = jnp.concatenate([w_qkv.T, w_out.T], axis=0)
    odd = lax.axis_index("group") % 2 == 1
    main = jnp.where(odd, cols[:, 64:], cols[:, :128])
    rest = jnp.where(odd, cols[:, :64], cols[:, 128:]).reshape(6, 2, 16, 64)
    rest = jnp.where(odd, rest[:, ::-1], rest)
    return main, jnp.concatenate([rest[:, 0], rest[:, 1]], axis=-1).reshape(PART, LANES)


WF = (2, 4, 4, 4, 2, 192, LANES)
WR = (2, 4, 4, 4, 2, PART, LANES)
WU = (4, 4, 4, 2, 192, LANES)
QKV = (18, TOK, 256)


def comm_sems():
    total = plan()[1]
    dma = pltpu.SemaphoreType.DMA
    return [dma((total,)), dma((total,)), dma((2, 16)), dma((2,))]


def gather_call(main, rest):
    return pl.pallas_call(
        gather_weights,
        out_shape=(jax.ShapeDtypeStruct(WF, jnp.bfloat16), jax.ShapeDtypeStruct(WR, jnp.bfloat16)),
        in_specs=[pl.BlockSpec(memory_space=pl.ANY)] * 2,
        out_specs=(pl.BlockSpec(memory_space=pl.ANY),) * 2,
        scratch_shapes=comm_sems(),
        compiler_params=pltpu.CompilerParams(collective_id=0, has_side_effects=True),
    )(main, rest)


def layer_kernel(lens, live, lat, tables, gain, wf_hbm, wr_hbm, out, wf, wr, wu, xs, qkv, att, sem):
    copies = [pltpu.make_async_copy(wr_hbm, wr, sem.at[0]), pltpu.make_async_copy(wf_hbm, wf, sem.at[1])]
    for copy in copies:
        copy.start()
    norm_tokens(lat, tables, gain, xs)
    copies[0].wait()
    unpack_rest(wr, wu)
    copies[1].wait()
    project(xs, wf, wu, qkv)
    attend(qkv, lens, att)
    finish(att, wf, wu, lat, lens, live, out)


def layer_call(lens, live, lat, tables, gain, wf, wr):
    smem = pl.BlockSpec(memory_space=pltpu.SMEM)
    vmem = pl.BlockSpec(memory_space=pltpu.VMEM)
    hbm = pl.BlockSpec(memory_space=pl.ANY)
    bf16 = jnp.bfloat16
    return pl.pallas_call(
        layer_kernel,
        out_shape=jax.ShapeDtypeStruct((TOK, D), bf16),
        in_specs=[smem, smem, vmem, vmem, vmem, hbm, hbm],
        out_specs=vmem,
        scratch_shapes=[pltpu.VMEM(WF, bf16), pltpu.VMEM(WR, bf16), pltpu.VMEM(WU, bf16), pltpu.VMEM((TOK, D), bf16),
                        pltpu.VMEM(QKV, bf16), pltpu.VMEM((6, TOK, 256), bf16), pltpu.SemaphoreType.DMA((2,))],
        compiler_params=pltpu.CompilerParams(vmem_limit_bytes=58 << 20),
    )(lens, live, lat, tables, gain, wf, wr)


def local(latents, window_index, window_len, live_blocks, norm_gain, w_qkv, w_out):
    main, rest = pack(w_qkv, w_out)
    wf, wr = gather_call(main, rest)
    out = layer_call(window_len, live_blocks, latents.reshape(TOK, D), window_tables(window_index),
                     norm_gain.reshape(1, D), wf, wr)
    return out.reshape(latents.shape)


def solution(mesh):
    in_specs = (
        P(("tile", "group"), None, None),
        P(("tile", "group")),
        P(("tile", "group")),
        P(("tile", "group")),
        P(),
        P("group", "tile"),
        P("group", "tile"),
    )
    out_specs = P(("tile", "group"), None, None)
    return jax.shard_map(local, mesh=mesh, in_specs=in_specs, out_specs=out_specs, check_vma=False)
```

time: 241 us -> 128 us (0.53)
  the two profiles are of different devices: /device:TPU:39 before, /device:TPU:1 now
where the time goes in v1:
time: 128 us
  Pallas kernels  120 us (94%)
  other arithmetic  5.84 us (5%)
  local copies, waits for them, and re-layouts  1.3 us (1%)
    pallas_call x1, Pallas kernels, gather_call(): pl.pallas_call(gather_weights, out_shape=(jax.ShapeDtypeStruct(WF, jnp.bf...  67.8 us
    pallas_call x1, Pallas kernels, layer_call(): pl.pallas_call(layer_kernel, out_shape=jax.ShapeDtypeStruct((TOK, D), bf1...  52.1 us

profile of v1, /device:TPU:1, one launch (start us, length us, event | category | flops | bytes accessed | tf_op | source)
XLA Modules:
  0.0 127.8 jit_solution(1663857861260490363)
XLA Ops:
  0.7 0.7 fusion.6
  1.3 1.3 %reshape.96.gain = f32[1,1536]{1,0:T(1,128)} reshape(f32[1536]{0:T(1024)} %param.11) | data formatting | bytes 12288 | tf_op jit(solution)/shard_map/reshape | solution.py:463
  2.6 0.1 iota_add_fusion
  2.7 1.6 %fusion.3.src_f = bf16[192,128]{1,0:T(8,128)(2,1)} fusion(bf16[144,192]{1,0:T(8,128)(2,1)} %bitcast.8, bf16[48,192]{1,0:T(8,128)(2,1)} %bitcast.11, pred[]{:T(512)S(6)} %eq.7), kind=kLoop, calls=%fused_computation.13 | loop fusion | flops 221184 | bytes 122881 | tf_op jit(solution)/shard_map/jit(_where)/select_n | solution.py:401
  4.3 0.8 fusion.1
  5.2 0.7 pad_maximum_fusion.2.src_r
  5.9 1.1 multiply_sine_fusion
  7.0 0.9 pad_maximum_fusion.tables
  7.8 67.8 %shard_map.73 = (bf16[2,4,4,4,2,192,128]{6,5,4,3,2,1,0:T(8,128)(2,1)}, bf16[2,4,4,4,2,96,128]{6,5,4,3,2,1,0:T(8,128)(2,1)}) custom-call(bf16[192,128]{1,0:T(8,128)(2,1)} %fusion.3.src_f, bf16[96,128]{1,0:T(8,128)(2,1)} %pad_maximum_fusion.2.src_r), custom_call_target="tpu_custom_call" | custom-call | tf_op jit(solution)/shard_map/pallas_call | solution.py:420
  75.7 52.1 %shard_map.74 = bf16[768,1536]{1,0:T(8,128)(2,1)} custom-call(s32[12]{0:T(128)} %lens.1, s32[1]{0:T(128)S(6)} %copy.10.live, bf16[768,1536]{1,0:T(8,128)(2,1)} %bitcast.7, f32[2,12,8,768]{3,2,1,0:T(8,128)} %pad_maximum_fusion.tables, f32[1,1536]{1,0:T(1,128)} %reshape.96.gain, bf16[2,4,4,4,2,192,128]{6,5,4,3,2,1,0:T(8,128)(2,1)} %get-tuple-element.7.wf_hbm, ...), custom_call_target="tpu_custom_call" | custom-call | tf_op jit(solution)/shard_map/pallas_call | solution.py:448
  (5 shorter events, 0.0 us)

commit v2 on v1

--- a/solution.py
+++ b/solution.py
@@ -157,7 +157,7 @@
     return ref_f.at[pl.ds(0 if color == "B" else PART, PART), :]
 
 
-def gather_weights(src_f, src_r, wf, wr, send_sem, recv_sem, sib_sem, loc_sem, meanwhile=None):
+def gather_weights(wq, wo, wf, wr, send_sem, recv_sem, sib_sem, meanwhile):
     tile = lax.axis_index("tile"); group = lax.axis_index("group")
     y = tile // 8; zh = (tile // 2) % 4; c = tile % 2
     zl = group // 4; x = group % 4
@@ -180,6 +180,7 @@
             table[axis, step] = dev_of(axis, step)
         return table[axis, step]
 
+    pack(wq, wo, group % 2, wf.at[zl, x, y, zh, c], wr.at[zl, x, y, zh, c])
     bar = pltpu.get_barrier_semaphore()
     peers = [("x", 1), ("x", 3), ("x", 2), ("y", 1), ("y", 3), ("z", 1), ("z", 7), ("c", 1)]
     for p in peers:
@@ -188,10 +189,6 @@
 
     own_f = wf.at[zl, x, y, zh, c]
     own_r = wr.at[zl, x, y, zh, c]
-    loc_f = pltpu.make_async_copy(src_f, own_f, loc_sem.at[0])
-    loc_r = pltpu.make_async_copy(src_r, own_r, loc_sem.at[1])
-    loc_f.start()
-    loc_r.start()
 
     def view(color, region, half=None, core=None):
         rx, ry, rz = region
@@ -217,8 +214,7 @@
         else:
             ident, color, region, axis, step, half = item
             if region == (0, 0, 0):
-                ref = parts_of(src_f, src_r, color)
-                dst = parts_of(own_f, own_r, color)
+                ref = dst = parts_of(own_f, own_r, color)
             else:
                 ref = dst = view(color, region, half)
             cp = pltpu.make_async_remote_copy(src_ref=ref, dst_ref=dst, send_sem=send_sem.at[ident], recv_sem=recv_sem.at[ident],
@@ -233,11 +229,8 @@
                                          device_id=dev("c", 1), device_id_type=MESH).wait_recv()
         for item in out:
             issue(item)
-        if n == 0:
-            loc_f.wait()
-            loc_r.wait()
-            if meanwhile is not None:
-                meanwhile()
+        if n in meanwhile:
+            meanwhile[n]()
     for i, (cp, color, region) in enumerate(sibs):
         ref = view(color, region, None, 1 - c)
         pltpu.make_async_remote_copy(src_ref=ref, dst_ref=ref, send_sem=sib_sem.at[0, i], recv_sem=sib_sem.at[1, i],
@@ -248,60 +241,51 @@
         cp.wait_send()
 
 
-def window_tables(window_index):
-    side = jnp.arange(WIN_SIDE, dtype=jnp.int32)
-    rows = (window_index // WIN_COLS * WIN_SIDE)[:, None] + side
-    cols = (window_index % WIN_COLS * WIN_SIDE)[:, None] + side
+def norm_block(b, index, lat, gain, xs_ref):
     quarter = D // 4
-    frequency = jnp.exp(jnp.arange(quarter, dtype=jnp.float32) * (-math.log(10000.0) / quarter))
-    angle = jnp.stack([rows, cols]).astype(jnp.float32)[..., None] * frequency
-    return jnp.concatenate([jnp.sin(angle), jnp.cos(angle)], axis=-1)
-
-
-def norm_tokens(lat, tables, gain, xs_ref):
-    def block(b, carry):
-        for h in range(2):
-            rows = pl.ds(pl.multiple_of(b * BLOCK + h * WIN_TOK, WIN_TOK), WIN_TOK)
-            win = 2 * b + h
-            tok = lat[rows, :].astype(jnp.float32)
-            half = D // 2
-            left = tok[:, :half].reshape(8, 8, half) + tables[0, win][:, None, :]
-            right = tok[:, half:].reshape(8, 8, half) + tables[1, win][None]
-            stream = jnp.concatenate([left.reshape(WIN_TOK, half), right.reshape(WIN_TOK, half)], axis=1)
-            scale = lax.rsqrt(jnp.mean(stream * stream, axis=-1, keepdims=True) + 1e-06)
-            xs_ref[rows, :] = (stream * scale * gain[...]).astype(jnp.bfloat16)
-        return carry
-
-    lax.fori_loop(0, SLOTS, block, 0)
-
-
-def coords(t):
-    return t // 8, (t // 2) % 4, t % 2
+    step = lax.broadcasted_iota(jnp.int32, (8, quarter), 1).astype(jnp.float32)
+    frequency = jnp.exp(step * (-math.log(10000.0) / quarter))
+    side = lax.broadcasted_iota(jnp.int32, (8, quarter), 0)
+    for h in range(2):
+        rows = slice(b * BLOCK + h * WIN_TOK, b * BLOCK + h * WIN_TOK + WIN_TOK)
+        place = index[2 * b + h]
+        table = []
+        for at in (lax.div(place, WIN_COLS), lax.rem(place, WIN_COLS)):
+            angle = (at * WIN_SIDE + side).astype(jnp.float32) * frequency
+            table.append(jnp.concatenate([jnp.sin(angle), jnp.cos(angle)], axis=1))
+        tok = lat[rows, :].astype(jnp.float32)
+        half = D // 2
+        left = tok[:, :half].reshape(8, 8, half) + table[0][:, None, :]
+        right = tok[:, half:].reshape(8, 8, half) + table[1][None]
+        stream = jnp.concatenate([left.reshape(WIN_TOK, half), right.reshape(WIN_TOK, half)], axis=1)
+        scale = lax.rsqrt(jnp.mean(stream * stream, axis=-1, keepdims=True) + 1e-06)
+        xs_ref[rows, :] = (stream * scale * gain[...]).astype(jnp.bfloat16)
 
 
 def unpack_rest(wr, wu):
     lane = lax.broadcasted_iota(jnp.int32, (PART, LANES), 1) < 64
 
-    def one(t, carry):
-        y, zh, c = coords(t)
-        for j in range(4):
-            zl, x = j // 2, (j % 2) * 2
-            even = wr[zl, x, y, zh, c].astype(jnp.float32)
-            odd = wr[zl, x + 1, y, zh, c].astype(jnp.float32)
-            low = jnp.where(lane, even, odd).astype(jnp.bfloat16)
-            high = pltpu.roll(jnp.where(lane, odd, even), 64, 1).astype(jnp.bfloat16)
-            for i in range(6):
-                wu[j, y, zh, c, 32 * i:32 * i + 16, :] = low[16 * i:16 * i + 16]
-                wu[j, y, zh, c, 32 * i + 16:32 * i + 32, :] = high[16 * i:16 * i + 16]
+    def one(y, carry):
+        for zh in range(4):
+            for c in range(2):
+                for j in range(4):
+                    zl, x = j // 2, (j % 2) * 2
+                    even = wr[zl, x, y, zh, c].astype(jnp.float32)
+                    odd = wr[zl, x + 1, y, zh, c].astype(jnp.float32)
+                    low = jnp.where(lane, even, odd).astype(jnp.bfloat16)
+                    high = pltpu.roll(jnp.where(lane, odd, even), 64, 1).astype(jnp.bfloat16)
+                    for i in range(6):
+                        wu[j, y, zh, c, 32 * i:32 * i + 16, :] = low[16 * i:16 * i + 16]
+                        wu[j, y, zh, c, 32 * i + 16:32 * i + 32, :] = high[16 * i:16 * i + 16]
         return carry
 
-    lax.fori_loop(0, 32, one, 0)
-
-
-def column_tile(wf, wu, groups):
+    lax.fori_loop(0, 4, one, 0)
+
+
+def column_tile(wf, wu, first, groups):
     spots = []
     for t, r in groups:
-        spots.append(coords(t) + (pl.ds(pl.multiple_of(r, 16), 16),))
+        spots.append((first + t // 8, (t // 2) % 4, t % 2, slice(r, r + 16)))
     tiles = []
     for k in range(12):
         j, kind = k // 3, k % 3
@@ -322,19 +306,18 @@
     c = lax.broadcasted_iota(jnp.int32, (256, 256), 1) // HEAD_DIM
     ones = jnp.where(r == c, 1.0, 0.0).astype(jnp.bfloat16)
 
-    def tile(n, carry):
-        groups = []
-        for i in range(16):
-            g = n * 16 + i
-            groups.append((g // 9, (g % 9) * 16))
-        p = lax.dot_general(xs_ref[...], column_tile(wf, wu, groups), NT, preferred_element_type=jnp.float32)
-        total = jnp.dot((p * p).astype(jnp.bfloat16), ones, preferred_element_type=jnp.float32)
-        extra = jnp.where(n < 6, HEAD_DIM ** -0.5, 1.0)
-        factor = jnp.where(n < 12, lax.rsqrt(total * (1.0 / HEAD_DIM) + 1e-06) * extra, 1.0)
-        qkv[n] = (p * factor).astype(jnp.bfloat16)
+    def half(m, carry):
+        for s in range(9):
+            groups = [((s * 16 + i) // 9, (s * 16 + i) % 9 * 16) for i in range(16)]
+            n = 9 * m + s
+            p = lax.dot_general(xs_ref[...], column_tile(wf, wu, 2 * m, groups), NT, preferred_element_type=jnp.float32)
+            total = jnp.dot((p * p).astype(jnp.bfloat16), ones, preferred_element_type=jnp.float32)
+            extra = jnp.where(n < 6, HEAD_DIM ** -0.5, 1.0)
+            factor = jnp.where(n < 12, lax.rsqrt(total * (1.0 / HEAD_DIM) + 1e-06) * extra, 1.0)
+            qkv[n] = (p * factor).astype(jnp.bfloat16)
         return carry
 
-    lax.fori_loop(0, 18, tile, 0)
+    lax.fori_loop(0, 2, half, 0)
 
 
 def attend(qkv, lens, att):
@@ -351,8 +334,10 @@
         high = jnp.where(query < 64, first, 64 + second)
         mask = jnp.where(key >= low, 1.0, 0.0) * jnp.where(key < high, 1.0, 0.0)
 
-        def pair(h, inner):
-            for part in range(2):
+        def pair(step, inner):
+            for i in range(4):
+                h = 2 * step + i // 2
+                part = i % 2
                 cols = slice(part * LANES, part * LANES + LANES)
                 q = qkv[h, rows, cols]
                 k = qkv[6 + h, rows, cols]
@@ -366,7 +351,7 @@
                 att[h, rows, cols] = (mixed[:, :LANES] / mixed[:, LANES:]).astype(jnp.bfloat16)
             return inner
 
-        lax.fori_loop(0, 6, pair, 0)
+        lax.fori_loop(0, 3, pair, 0)
         return carry
 
     lax.fori_loop(0, SLOTS, block, 0)
@@ -375,33 +360,38 @@
 def finish(att, wf, wu, lat, lens, live, out):
     tok = lax.broadcasted_iota(jnp.int32, (BLOCK, 256), 0)
 
-    def tile(n, carry):
-        groups = []
-        for i in range(16):
-            g = n * 16 + i
-            groups.append((g // 3, 144 + (g % 3) * 16))
-        wide = jnp.concatenate([att[h] for h in range(6)], axis=1)
-        update = lax.dot_general(wide, column_tile(wf, wu, groups), NT, preferred_element_type=jnp.float32)
-        cols = pl.ds(pl.multiple_of(n * 256, 256), 256)
-        for b in range(SLOTS):
-            base = lat[b * BLOCK:(b + 1) * BLOCK, cols].astype(jnp.float32)
-            first, second = lens[2 * b], lens[2 * b + 1]
-            limit = jnp.where(tok < 64, first, 64 + second)
-            limit = jnp.where(b < live[0], limit, 0)
-            moved_rows = update[b * BLOCK:(b + 1) * BLOCK]
-            out[b * BLOCK:(b + 1) * BLOCK, cols] = jnp.where(tok < limit, base + moved_rows, base).astype(jnp.bfloat16)
+    def half(m, carry):
+        for s in range(3):
+            groups = [((s * 16 + i) // 3, 144 + (s * 16 + i) % 3 * 16) for i in range(16)]
+            wide = jnp.concatenate([att[h] for h in range(6)], axis=1)
+            update = lax.dot_general(wide, column_tile(wf, wu, 2 * m, groups), NT, preferred_element_type=jnp.float32)
+            cols = pl.ds(pl.multiple_of(m * 768 + s * 256, 256), 256)
+            for b in range(SLOTS):
+                base = lat[b * BLOCK:(b + 1) * BLOCK, cols].astype(jnp.float32)
+                first, second = lens[2 * b], lens[2 * b + 1]
+                limit = jnp.where(tok < 64, first, 64 + second)
+                limit = jnp.where(b < live[0], limit, 0)
+                added = update[b * BLOCK:(b + 1) * BLOCK]
+                out[b * BLOCK:(b + 1) * BLOCK, cols] = jnp.where(tok < limit, base + added, base).astype(jnp.bfloat16)
         return carry
 
-    lax.fori_loop(0, 6, tile, 0)
-
-
-def pack(w_qkv, w_out):
-    cols = jnp.concatenate([w_qkv.T, w_out.T], axis=0)
-    odd = lax.axis_index("group") % 2 == 1
-    main = jnp.where(odd, cols[:, 64:], cols[:, :128])
-    rest = jnp.where(odd, cols[:, :64], cols[:, 128:]).reshape(6, 2, 16, 64)
-    rest = jnp.where(odd, rest[:, ::-1], rest)
-    return main, jnp.concatenate([rest[:, 0], rest[:, 1]], axis=-1).reshape(PART, LANES)
+    lax.fori_loop(0, 2, half, 0)
+
+
+def pack(wq, wo, odd, main, rest):
+    cols = jnp.concatenate([wq[...], wo[...]], axis=0).astype(jnp.float32)
+    low = lax.broadcasted_iota(jnp.int32, (2 * PART, LANES), 1) < 64
+    head = cols[:, :LANES]
+    turned = pltpu.roll(head, 64, 1)
+    last = cols[:, LANES:]
+    last = jnp.concatenate([last, last], axis=1)
+    pick = odd.astype(jnp.float32)
+    main[...] = jnp.where(pick > 0.5, jnp.where(low, turned, last), head).astype(jnp.bfloat16)
+    other = jnp.where(pick > 0.5, jnp.where(low, head, turned), last)
+    side = lax.broadcasted_iota(jnp.int32, (16, LANES), 1) // 64
+    for i in range(6):
+        a, b = other[32 * i:32 * i + 16], other[32 * i + 16:32 * i + 32]
+        rest[16 * i:16 * i + 16, :] = jnp.where(side == odd, a, b).astype(jnp.bfloat16)
 
 
 WF = (2, 4, 4, 4, 2, 192, LANES)
@@ -413,54 +403,36 @@
 def comm_sems():
     total = plan()[1]
     dma = pltpu.SemaphoreType.DMA
-    return [dma((total,)), dma((total,)), dma((2, 16)), dma((2,))]
-
-
-def gather_call(main, rest):
-    return pl.pallas_call(
-        gather_weights,
-        out_shape=(jax.ShapeDtypeStruct(WF, jnp.bfloat16), jax.ShapeDtypeStruct(WR, jnp.bfloat16)),
-        in_specs=[pl.BlockSpec(memory_space=pl.ANY)] * 2,
-        out_specs=(pl.BlockSpec(memory_space=pl.ANY),) * 2,
-        scratch_shapes=comm_sems(),
-        compiler_params=pltpu.CompilerParams(collective_id=0, has_side_effects=True),
-    )(main, rest)
-
-
-def layer_kernel(lens, live, lat, tables, gain, wf_hbm, wr_hbm, out, wf, wr, wu, xs, qkv, att, sem):
-    copies = [pltpu.make_async_copy(wr_hbm, wr, sem.at[0]), pltpu.make_async_copy(wf_hbm, wf, sem.at[1])]
-    for copy in copies:
-        copy.start()
-    norm_tokens(lat, tables, gain, xs)
-    copies[0].wait()
+    return [dma((total,)), dma((total,)), dma((2, 16))]
+
+
+def layer_kernel(index, lens, live, lat, gain, wq, wo, out, wf, wr, wu, xs, qkv, att, *sems):
+    chunk = {60 + 10 * b: (lambda b=b: norm_block(b, index, lat, gain, xs)) for b in range(SLOTS)}
+    gather_weights(wq, wo, wf, wr, *sems, chunk)
     unpack_rest(wr, wu)
-    copies[1].wait()
     project(xs, wf, wu, qkv)
     attend(qkv, lens, att)
     finish(att, wf, wu, lat, lens, live, out)
 
 
-def layer_call(lens, live, lat, tables, gain, wf, wr):
+def layer_call(index, lens, live, lat, gain, wq, wo):
     smem = pl.BlockSpec(memory_space=pltpu.SMEM)
     vmem = pl.BlockSpec(memory_space=pltpu.VMEM)
-    hbm = pl.BlockSpec(memory_space=pl.ANY)
     bf16 = jnp.bfloat16
     return pl.pallas_call(
         layer_kernel,
         out_shape=jax.ShapeDtypeStruct((TOK, D), bf16),
-        in_specs=[smem, smem, vmem, vmem, vmem, hbm, hbm],
+        in_specs=[smem, smem, smem, vmem, vmem, vmem, vmem],
         out_specs=vmem,
         scratch_shapes=[pltpu.VMEM(WF, bf16), pltpu.VMEM(WR, bf16), pltpu.VMEM(WU, bf16), pltpu.VMEM((TOK, D), bf16),
-                        pltpu.VMEM(QKV, bf16), pltpu.VMEM((6, TOK, 256), bf16), pltpu.SemaphoreType.DMA((2,))],
-        compiler_params=pltpu.CompilerParams(vmem_limit_bytes=58 << 20),
-    )(lens, live, lat, tables, gain, wf, wr)
+                        pltpu.VMEM(QKV, bf16), pltpu.VMEM((6, TOK, 256), bf16)] + comm_sems(),
+        compiler_params=pltpu.CompilerParams(collective_id=0, has_side_effects=True, vmem_limit_bytes=58 << 20),
+    )(index, lens, live, lat, gain, wq, wo)
 
 
 def local(latents, window_index, window_len, live_blocks, norm_gain, w_qkv, w_out):
-    main, rest = pack(w_qkv, w_out)
-    wf, wr = gather_call(main, rest)
-    out = layer_call(window_len, live_blocks, latents.reshape(TOK, D), window_tables(window_index),
-                     norm_gain.reshape(1, D), wf, wr)
+    out = layer_call(window_index, window_len, live_blocks, latents.reshape(TOK, D), norm_gain.reshape(1, D),
+                     w_qkv.T, w_out.T)
     return out.reshape(latents.shape)
 
 

time: 128 us -> 110 us (0.86)
  Pallas kernels: 120 us -> 105 us
  other arithmetic: 5.84 us -> 0 us
  local copies, waits for them, and re-layouts: 1.3 us -> 4.62 us
    pallas_call x1 -> x0, Pallas kernels: 67.8 us -> none  [gather_call(): pl.pallas_call(gather_weights, out_shape=(jax.ShapeDtypeStruct(WF, jnp.bf...]
    pallas_call x1, Pallas kernels: 52.1 us -> 105 us  [layer_call(): pl.pallas_call(layer_kernel, out_shape=jax.ShapeDtypeStruct((TOK, D), bf1...]
    unnamed x0 -> x1, local copies, waits for them, and re-layouts: none -> 3.32 us
    select_n x3 -> x0, other arithmetic: 2.42 us -> none  [the longest x1 1.6 us: pack(): main = jnp.where(odd, cols[:, 64:], cols[:, :128])]
    concatenate x2 -> x0, other arithmetic: 1.57 us -> none  [the longest x1 0.87 us: window_tables(): return jnp.concatenate([jnp.sin(angle), jnp.cos(angle)], axis=-1)]
where the time goes in v2:
time: 110 us
  Pallas kernels  105 us (95%)
  local copies, waits for them, and re-layouts  4.62 us (4%)
    pallas_call x1, Pallas kernels, layer_call(): pl.pallas_call(layer_kernel, out_shape=jax.ShapeDtypeStruct((TOK, D), bf1...  105 us
    unnamed x1, local copies, waits for them, and re-layouts  3.32 us

profile of v2, /device:TPU:1, one launch (start us, length us, event | category | flops | bytes accessed | tf_op | source)
XLA Modules:
  0.0 109.9 jit_solution(17551468125827974092)
XLA Ops:
  0.7 1.3 %reshape.10.gain = f32[1,1536]{1,0:T(1,128)} reshape(f32[1536]{0:T(1024)} %param.11) | data formatting | bytes 12288 | tf_op jit(solution)/shard_map/reshape | solution.py:434
  1.9 104.6 %shard_map.73 = bf16[768,1536]{1,0:T(8,128)(2,1)} custom-call(s32[12]{0:T(128)} %index.1, s32[12]{0:T(128)} %lens.1, s32[1]{0:T(128)S(6)} %copy.9.live, bf16[768,1536]{1,0:T(8,128)(2,1)} %bitcast.5, f32[1,1536]{1,0:T(1,128)} %reshape.10.gain, bf16[144,192]{1,0:T(8,128)(2,1)} %bitcast.6, bf16[48,192]{1,0:T(8,128)(2,1)} %bitcast.7), custom_call_target="tpu_custom_call" | custom-call | tf_op jit(solution)/shard_map/pallas_call | solution.py:422
  106.6 3.3 %copy.10 = bf16[6,128,1536]{2,1,0:T(8,128)(2,1)} copy(bf16[6,128,1536]{2,1,0:T(8,128)(2,1)} %bitcast.4) | data formatting | bytes 4718592

commit v3 on v2

--- a/solution.py
+++ b/solution.py
@@ -247,7 +247,7 @@
     frequency = jnp.exp(step * (-math.log(10000.0) / quarter))
     side = lax.broadcasted_iota(jnp.int32, (8, quarter), 0)
     for h in range(2):
-        rows = slice(b * BLOCK + h * WIN_TOK, b * BLOCK + h * WIN_TOK + WIN_TOK)
+        rows = pl.ds(pl.multiple_of(b * BLOCK + h * WIN_TOK, WIN_TOK), WIN_TOK)
         place = index[2 * b + h]
         table = []
         for at in (lax.div(place, WIN_COLS), lax.rem(place, WIN_COLS)):
@@ -259,7 +259,8 @@
         right = tok[:, half:].reshape(8, 8, half) + table[1][None]
         stream = jnp.concatenate([left.reshape(WIN_TOK, half), right.reshape(WIN_TOK, half)], axis=1)
         scale = lax.rsqrt(jnp.mean(stream * stream, axis=-1, keepdims=True) + 1e-06)
-        xs_ref[rows, :] = (stream * scale * gain[...]).astype(jnp.bfloat16)
+        wide = jnp.concatenate([gain[k:k + 1, :] for k in range(D // LANES)], axis=1)
+        xs_ref[rows, :] = (stream * scale * wide).astype(jnp.bfloat16)
 
 
 def unpack_rest(wr, wu):
@@ -285,7 +286,12 @@
 def column_tile(wf, wu, first, groups):
     spots = []
     for t, r in groups:
-        spots.append((first + t // 8, (t // 2) % 4, t % 2, slice(r, r + 16)))
+        if isinstance(t, int):
+            spots.append((first + t // 8, (t // 2) % 4, t % 2, slice(r, r + 16)))
+        else:
+            half = lax.div(t, 2)
+            y = lax.div(t, 8)
+            spots.append((y, half - 4 * y, t - 2 * half, pl.ds(pl.multiple_of(r, 16), 16)))
     tiles = []
     for k in range(12):
         j, kind = k // 3, k % 3
@@ -306,18 +312,22 @@
     c = lax.broadcasted_iota(jnp.int32, (256, 256), 1) // HEAD_DIM
     ones = jnp.where(r == c, 1.0, 0.0).astype(jnp.bfloat16)
 
-    def half(m, carry):
-        for s in range(9):
-            groups = [((s * 16 + i) // 9, (s * 16 + i) % 9 * 16) for i in range(16)]
-            n = 9 * m + s
-            p = lax.dot_general(xs_ref[...], column_tile(wf, wu, 2 * m, groups), NT, preferred_element_type=jnp.float32)
-            total = jnp.dot((p * p).astype(jnp.bfloat16), ones, preferred_element_type=jnp.float32)
-            extra = jnp.where(n < 6, HEAD_DIM ** -0.5, 1.0)
-            factor = jnp.where(n < 12, lax.rsqrt(total * (1.0 / HEAD_DIM) + 1e-06) * extra, 1.0)
-            qkv[n] = (p * factor).astype(jnp.bfloat16)
+    def tile(n, carry):
+        t0 = lax.div(16 * n, 9)
+        r0 = 16 * n - 9 * t0
+        groups = []
+        for i in range(16):
+            r = r0 + i
+            over = (r >= 9).astype(jnp.int32) + (r >= 18).astype(jnp.int32)
+            groups.append((t0 + over, 16 * (r - 9 * over)))
+        p = lax.dot_general(xs_ref[...], column_tile(wf, wu, 0, groups), NT, preferred_element_type=jnp.float32)
+        total = jnp.dot((p * p).astype(jnp.bfloat16), ones, preferred_element_type=jnp.float32)
+        extra = jnp.where(n < 6, HEAD_DIM ** -0.5, 1.0)
+        factor = jnp.where(n < 12, lax.rsqrt(total * (1.0 / HEAD_DIM) + 1e-06) * extra, 1.0)
+        qkv[n] = (p * factor).astype(jnp.bfloat16)
         return carry
 
-    lax.fori_loop(0, 2, half, 0)
+    lax.fori_loop(0, 18, tile, 0)
 
 
 def attend(qkv, lens, att):
@@ -406,8 +416,18 @@
     return [dma((total,)), dma((total,)), dma((2, 16))]
 
 
-def layer_kernel(index, lens, live, lat, gain, wq, wo, out, wf, wr, wu, xs, qkv, att, *sems):
-    chunk = {60 + 10 * b: (lambda b=b: norm_block(b, index, lat, gain, xs)) for b in range(SLOTS)}
+def norm_tokens(index, lat, gain, xs):
+    def block(b, carry):
+        norm_block(b, index, lat, gain, xs)
+        return carry
+
+    lax.fori_loop(0, SLOTS, block, 0)
+
+
+def layer_kernel(index, lens, live, lat_hbm, gain, wq, wo, out, wf, wr, wu, xs, qkv, att, lat, lat_sem, *sems):
+    fetch = pltpu.make_async_copy(lat_hbm, lat, lat_sem)
+    fetch.start()
+    chunk = {50: fetch.wait, 100: lambda: norm_tokens(index, lat, gain, xs)}
     gather_weights(wq, wo, wf, wr, *sems, chunk)
     unpack_rest(wr, wu)
     project(xs, wf, wu, qkv)
@@ -421,17 +441,18 @@
     bf16 = jnp.bfloat16
     return pl.pallas_call(
         layer_kernel,
-        out_shape=jax.ShapeDtypeStruct((TOK, D), bf16),
-        in_specs=[smem, smem, smem, vmem, vmem, vmem, vmem],
+        out_shape=pltpu.VMEM((TOK, D), bf16),
+        in_specs=[smem, smem, smem, pl.BlockSpec(memory_space=pl.ANY), vmem, vmem, vmem],
         out_specs=vmem,
         scratch_shapes=[pltpu.VMEM(WF, bf16), pltpu.VMEM(WR, bf16), pltpu.VMEM(WU, bf16), pltpu.VMEM((TOK, D), bf16),
-                        pltpu.VMEM(QKV, bf16), pltpu.VMEM((6, TOK, 256), bf16)] + comm_sems(),
+                        pltpu.VMEM(QKV, bf16), pltpu.VMEM((6, TOK, 256), bf16),
+                        pltpu.VMEM((TOK, D), bf16), pltpu.SemaphoreType.DMA] + comm_sems(),
         compiler_params=pltpu.CompilerParams(collective_id=0, has_side_effects=True, vmem_limit_bytes=58 << 20),
     )(index, lens, live, lat, gain, wq, wo)
 
 
 def local(latents, window_index, window_len, live_blocks, norm_gain, w_qkv, w_out):
-    out = layer_call(window_index, window_len, live_blocks, latents.reshape(TOK, D), norm_gain.reshape(1, D),
+    out = layer_call(window_index, window_len, live_blocks, latents.reshape(TOK, D), norm_gain.reshape(D // LANES, LANES),
                      w_qkv.T, w_out.T)
     return out.reshape(latents.shape)
 

time: 110 us -> 103 us (0.936)
  Pallas kernels: 105 us -> 100 us
  local copies, waits for them, and re-layouts: 4.62 us -> 1.41 us
    pallas_call x1, Pallas kernels: 105 us -> 100 us  [layer_call(): pl.pallas_call(layer_kernel, out_shape=pltpu.VMEM((TOK, D), bf16), in_spe...]
    unnamed x1, local copies, waits for them, and re-layouts: 3.32 us -> 1.41 us
    reshape x1 -> x0, local copies, waits for them, and re-layouts: 1.29 us -> none  [local(): norm_gain.reshape(1, D)]
where the time goes in v3:
time: 103 us; the launch traced here: 102 us
  Pallas kernels  100 us (97%)
  local copies, waits for them, and re-layouts  1.41 us (1%)
    pallas_call x1, Pallas kernels, layer_call(): pl.pallas_call(layer_kernel, out_shape=pltpu.VMEM((TOK, D), bf16), in_spe...  100 us

profile of v3, /device:TPU:1, one launch (start us, length us, event | category | flops | bytes accessed | tf_op | source)
XLA Modules:
  0.0 102.4 jit_solution(14157038001750431440)
XLA Ops:
  0.7 100.4 %shard_map.73 = bf16[768,1536]{1,0:T(8,128)(2,1)S(1)} custom-call(s32[12]{0:T(128)} %index.1, s32[12]{0:T(128)} %lens.1, s32[1]{0:T(128)S(6)} %copy.10.live, bf16[768,1536]{1,0:T(8,128)(2,1)} %bitcast.6, f32[12,128]{1,0:T(8,128)} %bitcast.9, bf16[144,192]{1,0:T(8,128)(2,1)} %bitcast.7, bf16[48,192]{1,0:T(8,128)(2,1)} %bitcast.8), custom_call_target="tpu_custom_call" | custom-call | tf_op jit(solution)/shard_map/pallas_call | solution.py:442
  101.0 1.4 %copy.9 = bf16[6,128,1536]{2,1,0:T(8,128)(2,1)} copy(bf16[6,128,1536]{2,1,0:T(8,128)(2,1)S(1)} %bitcast.5) | data formatting | bytes 4718592

commit v4 on v3

--- a/solution.py
+++ b/solution.py
@@ -45,7 +45,7 @@
         for r in region:
             if r == FULL:
                 n *= 4
-        return n // 2 if half else n
+        return n if half is None else n // 2
 
     def send(now, color, region, axis, step, half=None):
         n = AXLEN[axis]
@@ -58,7 +58,7 @@
         ident = count[0]
         count[0] += 1
         seq[0] += 1
-        heapq.heappush(queue, (end + 1.0 + 0.75 * hops, seq[0], ident, color, moved(region, axis, step), half))
+        heapq.heappush(queue, (end + 2.2 + 0.75 * hops, seq[0], ident, color, moved(region, axis, step), half))
         return (ident, color, region, axis, step, half)
 
     def complete(now, color, region, out):
@@ -126,7 +126,9 @@
             out.append(send(now, color, region, last, 3, 1))
         key = (color, region[l])
         have[key] = have.get(key, 0) + 1
-        if have[key] == 8:
+        if region[l] == 2:
+            out.append(("sib", color, region))
+        elif have[key] == 8:
             out.append(("sib", color, (region[0], region[1], FULL)))
 
     first = []
@@ -235,10 +237,7 @@
         ref = view(color, region, None, 1 - c)
         pltpu.make_async_remote_copy(src_ref=ref, dst_ref=ref, send_sem=sib_sem.at[0, i], recv_sem=sib_sem.at[1, i],
                                      device_id=dev("c", 1), device_id_type=MESH).wait_recv()
-    for cp in sends:
-        cp.wait_send()
-    for cp, _, _ in sibs:
-        cp.wait_send()
+    return sends + [cp for cp, _, _ in sibs]
 
 
 def norm_block(b, index, lat, gain, xs_ref):
@@ -413,7 +412,7 @@
 def comm_sems():
     total = plan()[1]
     dma = pltpu.SemaphoreType.DMA
-    return [dma((total,)), dma((total,)), dma((2, 16))]
+    return [dma((total,)), dma((total,)), dma((2, 32))]
 
 
 def norm_tokens(index, lat, gain, xs):
@@ -428,11 +427,13 @@
     fetch = pltpu.make_async_copy(lat_hbm, lat, lat_sem)
     fetch.start()
     chunk = {50: fetch.wait, 100: lambda: norm_tokens(index, lat, gain, xs)}
-    gather_weights(wq, wo, wf, wr, *sems, chunk)
+    sent = gather_weights(wq, wo, wf, wr, *sems, chunk)
     unpack_rest(wr, wu)
     project(xs, wf, wu, qkv)
     attend(qkv, lens, att)
     finish(att, wf, wu, lat, lens, live, out)
+    for cp in sent:
+        cp.wait_send()
 
 
 def layer_call(index, lens, live, lat, gain, wq, wo):

time: 103 us -> 96.8 us (0.940)
  Pallas kernels: 100 us -> 94.6 us
    pallas_call x1, Pallas kernels: 100 us -> 94.6 us  [layer_call(): pl.pallas_call(layer_kernel, out_shape=pltpu.VMEM((TOK, D), bf16), in_spe...]
where the time goes in v4:
time: 96.8 us; the launch traced here: 96.7 us
  Pallas kernels  94.6 us (98%)
  local copies, waits for them, and re-layouts  1.41 us (1%)
    pallas_call x1, Pallas kernels, layer_call(): pl.pallas_call(layer_kernel, out_shape=pltpu.VMEM((TOK, D), bf16), in_spe...  94.6 us

profile of v4, /device:TPU:1, one launch (start us, length us, event | category | flops | bytes accessed | tf_op | source)
XLA Modules:
  0.0 96.7 jit_solution(3983226739924344418)
XLA Ops:
  0.7 94.6 %shard_map.73 = bf16[768,1536]{1,0:T(8,128)(2,1)S(1)} custom-call(s32[12]{0:T(128)} %index.1, s32[12]{0:T(128)} %lens.1, s32[1]{0:T(128)S(6)} %copy.10.live, bf16[768,1536]{1,0:T(8,128)(2,1)} %bitcast.6, f32[12,128]{1,0:T(8,128)} %bitcast.9, bf16[144,192]{1,0:T(8,128)(2,1)} %bitcast.7, bf16[48,192]{1,0:T(8,128)(2,1)} %bitcast.8), custom_call_target="tpu_custom_call" | custom-call | tf_op jit(solution)/shard_map/pallas_call | solution.py:443
  95.3 1.4 %copy.9 = bf16[6,128,1536]{2,1,0:T(8,128)(2,1)} copy(bf16[6,128,1536]{2,1,0:T(8,128)(2,1)S(1)} %bitcast.5) | data formatting | bytes 4718592
